TPU v7x, 256 devices: a whole 4x4x8 slice. The times are simulated.
256 devices in a mesh: expert: 64 (over z, x, core), tensor: 4 (over y).
Axes of the slice: x: 4, y: 4, z: 8, core: 2. Of those that a mesh axis runs over, the one named last changes fastest.
Arguments:
- tokens: bfloat16 [16384, 2048], P('expert', 'tensor'), may hold values from -6 to 6
- out_grads: bfloat16 [16384, 2048], P('expert', 'tensor'), may hold values from -6 to 6
- species: int32 [16384, 1], P('expert'), may hold values from 0 to 63; in each aligned block of 64 rows (0 to 63, 64 to 127, ...) at most 2 rows name the same one
- expert_table: int32 [64], replicated, may hold values from 0 to 63, each once
- gate_weight: bfloat16 [64, 2048, 4096], P('expert', None, 'tensor'), may hold values from -0.125 to 0.125
- up_weight: bfloat16 [64, 2048, 4096], P('expert', None, 'tensor'), may hold values from -0.125 to 0.125
- down_weight: bfloat16 [64, 4096, 2048], P('expert', 'tensor'), may hold values from -0.09375 to 0.09375
Outputs:
- token_grads: bfloat16 [16384, 2048], P('expert', 'tensor')
Inputs may be any that keep to these rules, and one draw needn't show every extreme that they name: In each aligned block of 64 rows no species occurs more than 2 times, and in some blocks one species occurs exactly 2 times. `expert_table`: each species has a different expert.
All inputs are finite; a program needn't handle non-finite values.
Results may differ from a plain program's by a relative error of at most 0.0095.
Values may be sent and summed in bfloat16 or wider, within the bound.
A program may use at most 64 MiB of HBM per device.

v0:
```python
import jax
import jax.numpy as jnp
from jax import lax
from jax.sharding import PartitionSpec as P


def expert_partial(expert_rows, expert_grads, gate_matrix, up_matrix, down_matrix):
    contract = (((1,), (1,)), ((), ()))
    gate_pre = jnp.dot(expert_rows, gate_matrix, preferred_element_type=jnp.float32)
    up_pre = jnp.dot(expert_rows, up_matrix, preferred_element_type=jnp.float32)
    hidden_grad = lax.dot_general(
        expert_grads, down_matrix, contract, preferred_element_type=jnp.float32
    )
    sigmoid_gate = jax.nn.sigmoid(gate_pre)
    up_grad = (hidden_grad * gate_pre * sigmoid_gate).astype(jnp.bfloat16)
    gate_grad = (
        hidden_grad * up_pre * sigmoid_gate * (1.0 + gate_pre * (1.0 - sigmoid_gate))
    ).astype(jnp.bfloat16)
    partial_sum = lax.dot_general(
        gate_grad, gate_matrix, contract, preferred_element_type=jnp.float32
    )
    return partial_sum + lax.dot_general(
        up_grad, up_matrix, contract, preferred_element_type=jnp.float32
    )


def per_device(tokens, out_grads, species, expert_table, gate_weight, up_weight, down_weight):
    tensor_size = lax.axis_size("tensor")
    tensor_index = lax.axis_index("tensor")
    experts = expert_table.shape[0]
    group_tokens_count = tokens.shape[0]
    rows_dev = group_tokens_count // tensor_size
    head_width = tokens.shape[1]
    model_width = head_width * tensor_size
    capacity = 2 * rows_dev // experts
    expert_ids = jnp.arange(experts, dtype=jnp.int32)
    species_hits = species == expert_ids[None, :]
    expert_of = jnp.sum(jnp.where(species_hits, expert_table[None, :], 0), axis=1).reshape(
        tensor_size, rows_dev
    )
    onehot = (expert_of[:, :, None] == expert_ids[None, None, :]).astype(jnp.int32)
    earlier = jnp.cumsum(onehot, axis=1) - onehot
    slot_of = jnp.sum(earlier * onehot, axis=2)
    place_of = expert_of * capacity + slot_of
    slot_ids = jnp.arange(experts * capacity, dtype=jnp.int32)
    select = (slot_ids[None, :, None] == place_of[:, None, :]).astype(jnp.bfloat16)
    group_select = select.reshape(tensor_size, experts, capacity, rows_dev)
    own_select = lax.dynamic_index_in_dim(select, tensor_index, 0, keepdims=False)
    group_tokens, group_grads = (
        lax.all_gather(tokens, "tensor", axis=1, tiled=True),
        lax.all_gather(out_grads, "tensor", axis=1, tiled=True),
    )
    packed_rows = jnp.einsum(
        "tecr,trd->etcd",
        group_select,
        group_tokens.reshape(tensor_size, rows_dev, model_width),
        preferred_element_type=jnp.float32,
    ).astype(jnp.bfloat16)
    packed_grads = jnp.einsum(
        "tecr,trd->etcd",
        group_select,
        group_grads.reshape(tensor_size, rows_dev, model_width),
        preferred_element_type=jnp.float32,
    ).astype(jnp.bfloat16)
    packed_rows = packed_rows.reshape(experts, tensor_size * capacity, model_width)
    packed_grads = packed_grads.reshape(experts, tensor_size * capacity, model_width)
    expert_rows, expert_grads = (
        lax.all_to_all(packed_rows, "expert", split_axis=0, concat_axis=0, tiled=True),
        lax.all_to_all(packed_grads, "expert", split_axis=0, concat_axis=0, tiled=True),
    )
    slot_count = expert_rows.shape[0] * expert_rows.shape[1]
    partial_sum = expert_partial(
        expert_rows.reshape(slot_count, model_width),
        expert_grads.reshape(slot_count, model_width),
        gate_weight[0],
        up_weight[0],
        down_weight[0],
    )
    summed = lax.psum_scatter(
        partial_sum.reshape(experts, tensor_size * capacity, model_width).astype(jnp.bfloat16),
        "tensor",
        scatter_dimension=1,
        tiled=True,
    )
    returned = lax.all_to_all(summed, "expert", split_axis=0, concat_axis=0, tiled=True)
    own_grads = lax.dot_general(
        own_select,
        returned.reshape(experts * capacity, model_width),
        (((0,), (0,)), ((), ())),
        preferred_element_type=jnp.float32,
    ).astype(jnp.bfloat16)
    token_grads = lax.all_to_all(own_grads, "tensor", split_axis=1, concat_axis=0, tiled=True)
    return token_grads


def solution(mesh):
    placed = (
        P("expert", "tensor"),
        P("expert", "tensor"),
        P("expert", None),
        P(),
        P("expert", None, "tensor"),
        P("expert", None, "tensor"),
        P("expert", "tensor", None),
    )
    return jax.shard_map(
        per_device, mesh=mesh, in_specs=placed, out_specs=P("expert", "tensor"), check_vma=False
    )
```

profile of v0, /device:TPU:1, one launch (start us, length us, event | category | flops | bytes accessed | tf_op | source)
XLA Modules:
  0.0 264.5 jit_solution(15965972787222262756)
XLA Ops:
  6.5 0.7 all-gather.3.cloned.1.call-update
  7.3 0.8 select_reduce_fusion.1
  8.0 0.1 reshape.41
  8.1 0.1 fusion.33
  8.2 0.1 reduce_window_sum.11
  8.4 0.2 select_reduce_fusion
  8.6 28.9 %all-gather.3.cloned.1.call-done = bf16[256,2048]{1,0:T(8,128)(2,1)} async-done(((bf16[256,512]{1,0:T(8,128)(2,1)}), bf16[256,2048]{1,0:T(8,128)(2,1)}) %all-gather.3.cloned.1.call-update) | async-done | bytes 1048592 | tf_op jit(solution)/shard_map/all_gather | solution.py:51
  37.6 2.0 convolution_convert_fusion.1
  39.5 2.5 copy.26
  42.0 12.7 %all-to-all-start = ((bf16[64,8,2048]{2,1,0:T(8,128)(2,1)}), bf16[64,8,2048]{2,1,0:T(8,128)(2,1)S(1)}, u32[]{:S(2)}, u32[]{:S(2)}) async-start(bf16[64,8,2048]{2,1,0:T(8,128)(2,1)} %copy.26), calls=%async_computation | async-start | bytes 4194304 | tf_op jit(solution)/shard_map/all_to_all | solution.py:69
  54.7 0.0 all-gather.5.cloned.1.call-start
  54.8 0.7 all-gather.5.cloned.1.call-update
  55.5 26.7 %all-gather.5.cloned.1.call-done = bf16[256,2048]{1,0:T(8,128)(2,1)} async-done(((bf16[256,512]{1,0:T(8,128)(2,1)}), bf16[256,2048]{1,0:T(8,128)(2,1)}) %all-gather.5.cloned.1.call-update) | async-done | bytes 1048592 | tf_op jit(solution)/shard_map/all_gather | solution.py:50
  82.2 2.0 convolution_convert_fusion
  84.2 2.5 copy.27
  86.6 17.8 %all-to-all-done = bf16[64,8,2048]{2,1,0:T(8,128)(2,1)S(1)} async-done(((bf16[64,8,2048]{2,1,0:T(8,128)(2,1)}), bf16[64,8,2048]{2,1,0:T(8,128)(2,1)S(1)}, u32[]{:S(2)}, u32[]{:S(2)}) %all-to-all-start) | async-done | bytes 2097184 | tf_op jit(solution)/shard_map/all_to_all | solution.py:69
  104.4 7.2 %all-to-all-start.1 = ((bf16[64,8,2048]{2,1,0:T(8,128)(2,1)}), bf16[64,8,2048]{2,1,0:T(8,128)(2,1)}, u32[]{:S(2)}, u32[]{:S(2)}) async-start(bf16[64,8,2048]{2,1,0:T(8,128)(2,1)} %copy.27), calls=%async_computation.1 | async-start | bytes 4194304 | tf_op jit(solution)/shard_map/all_to_all | solution.py:68
  111.6 0.2 reduce-scatter.2.cloned.1.call-start
  111.8 6.0 %fusion.8 = f32[512,1024]{1,0:T(8,128)} fusion(bf16[1,1024,2048]{2,1,0:T(8,128)(2,1)} %param.13, bf16[64,8,2048]{2,1,0:T(8,128)(2,1)S(1)} %all-to-all-done), kind=kOutput, calls=%fused_computation.8 | convolution fusion | flops 2147483648 | bytes 8388608 | tf_op jit(solution)/shard_map/dot_general | solution.py:11
  117.8 43.4 %all-to-all-done.1 = bf16[64,8,2048]{2,1,0:T(8,128)(2,1)} async-done(((bf16[64,8,2048]{2,1,0:T(8,128)(2,1)}), bf16[64,8,2048]{2,1,0:T(8,128)(2,1)}, u32[]{:S(2)}, u32[]{:S(2)}) %all-to-all-start.1) | async-done | bytes 2097184 | tf_op jit(solution)/shard_map/all_to_all | solution.py:68
  161.2 6.5 %fusion.2 = f32[512,1024]{1,0:T(8,128)} fusion(bf16[1,2048,1024]{2,1,0:T(8,128)(2,1)} %param.11, bf16[64,8,2048]{2,1,0:T(8,128)(2,1)} %all-to-all-done.1), kind=kOutput, calls=%fused_computation.2 | convolution fusion | flops 2147483648 | bytes 8388608 | tf_op jit(solution)/shard_map/dot_general | solution.py:9
  167.7 11.5 %fusion = f32[512,2048]{1,0:T(8,128)} fusion(bf16[1,2048,1024]{2,1,0:T(8,128)(2,1)} %param.11, f32[512,1024]{1,0:T(8,128)} %fusion.2, f32[512,1024]{1,0:T(8,128)S(1)} %copy-done, bf16[1,2048,1024]{2,1,0:T(8,128)(2,1)} %param.12, bf16[64,8,2048]{2,1,0:T(8,128)(2,1)} %all-to-all-done.1), kind=kOutput, calls=%fused_computation | convolution fusion | flops 4300210176 | bytes 18874368 | tf_op jit(solution)/shard_map/dot_general | solution.py:19
  179.2 6.5 %fusion.12 = bf16[64,8,2048]{2,1,0:T(8,128)(2,1)S(1)} fusion(f32[512,2048]{1,0:T(8,128)} %fusion, bf16[1,2048,1024]{2,1,0:T(8,128)(2,1)} %param.12, f32[512,1024]{1,0:T(8,128)S(1)} %copy-done, f32[512,1024]{1,0:T(8,128)} %fusion.2), kind=kOutput, calls=%fused_computation.13 | convolution fusion | flops 2152726528 | bytes 14680064 | tf_op jit(solution)/shard_map/dot_general | solution.py:22
  185.7 2.5 copy.28
  188.2 29.1 %reduce-scatter.2.cloned.1.call-done = bf16[64,2,2048]{2,0,1:T(8,128)(2,1)} async-done(((bf16[64,8,2048]{2,0,1:T(8,128)(2,1)}), bf16[64,2,2048]{2,0,1:T(8,128)(2,1)}) %reduce-scatter.2.cloned.1.call-update) | async-done | bytes 524304 | tf_op jit(solution)/shard_map/reduce_scatter | solution.py:79
  217.3 2.4 copy.29
  219.7 10.7 %all-to-all-start.2 = ((bf16[64,2,2048]{2,1,0:T(2,128)(2,1)}), bf16[64,2,2048]{2,1,0:T(2,128)(2,1)S(1)}, u32[]{:S(2)}, u32[]{:S(2)}) async-start(bf16[64,2,2048]{2,1,0:T(2,128)(2,1)} %copy.29), calls=%async_computation.3 | async-start | bytes 1048576 | tf_op jit(solution)/shard_map/all_to_all | solution.py:85
  230.4 17.7 %all-to-all-done.2 = bf16[64,2,2048]{2,1,0:T(2,128)(2,1)S(1)} async-done(((bf16[64,2,2048]{2,1,0:T(2,128)(2,1)}), bf16[64,2,2048]{2,1,0:T(2,128)(2,1)S(1)}, u32[]{:S(2)}, u32[]{:S(2)}) %all-to-all-start.2) | async-done | bytes 524320 | tf_op jit(solution)/shard_map/all_to_all | solution.py:85
  248.1 0.2 reshape.48
  248.3 0.3 convolution_convert_fusion.2
  248.6 8.6 %all_to_all.34 = bf16[64,4,512]{2,0,1:T(8,128)(2,1)S(1)} all-to-all(bf16[64,4,512]{2,0,1:T(8,128)(2,1)S(1)} %bitcast.69), channel_id=1, replica_groups=mesh['expert'=64,'tensor'=4] {'tensor'}, dimensions={1} | all-to-all | bytes 524288 | tf_op jit(solution)/shard_map/all_to_all | solution.py:92
  257.2 0.7 copy.37
  (8 shorter events, 0.1 us)
Async XLA Ops:
  6.5 31.0 %all-gather.3.cloned.1.call-start = ((), (), s32[]{:S(2)}) async-start(), calls=%async_computation.5 | async-start | bytes 1310720 | tf_op jit(solution)/shard_map/all_gather | solution.py:51
  42.0 62.4 %all-to-all-start = ((bf16[64,8,2048]{2,1,0:T(8,128)(2,1)}), bf16[64,8,2048]{2,1,0:T(8,128)(2,1)S(1)}, u32[]{:S(2)}, u32[]{:S(2)}) async-start(bf16[64,8,2048]{2,1,0:T(8,128)(2,1)} %copy.26), calls=%async_computation | async-start | bytes 4194304 | tf_op jit(solution)/shard_map/all_to_all | solution.py:69
  54.7 27.4 %all-gather.5.cloned.1.call-start = ((), (), s32[]{:S(2)}) async-start(), calls=%async_computation.6 | async-start | bytes 1310720 | tf_op jit(solution)/shard_map/all_gather | solution.py:50
  104.4 56.8 %all-to-all-start.1 = ((bf16[64,8,2048]{2,1,0:T(8,128)(2,1)}), bf16[64,8,2048]{2,1,0:T(8,128)(2,1)}, u32[]{:S(2)}, u32[]{:S(2)}) async-start(bf16[64,8,2048]{2,1,0:T(8,128)(2,1)} %copy.27), calls=%async_computation.1 | async-start | bytes 4194304 | tf_op jit(solution)/shard_map/all_to_all | solution.py:68
  111.6 105.7 %reduce-scatter.2.cloned.1.call-start = ((), (), s32[]{:S(2)}) async-start(), calls=%async_computation.7 | async-start | bytes 2621440 | tf_op jit(solution)/shard_map/reduce_scatter | solution.py:79
  117.8 49.9 %copy-start = (f32[512,1024]{1,0:T(8,128)S(1)}, f32[512,1024]{1,0:T(8,128)}, u32[]{:S(2)}) copy-start(f32[512,1024]{1,0:T(8,128)} %fusion.8) | copy-start | bytes 6291460
  219.7 28.4 %all-to-all-start.2 = ((bf16[64,2,2048]{2,1,0:T(2,128)(2,1)}), bf16[64,2,2048]{2,1,0:T(2,128)(2,1)S(1)}, u32[]{:S(2)}, u32[]{:S(2)}) async-start(bf16[64,2,2048]{2,1,0:T(2,128)(2,1)} %copy.29), calls=%async_computation.3 | async-start | bytes 1048576 | tf_op jit(solution)/shard_map/all_to_all | solution.py:85
Sparse Core Ops, SparseCore 0:
  9.1 28.3 all-gather.2
  57.4 24.7 all-gather.4
  188.4 28.8 reduce-scatter.1
where the time goes:
time: 265 us; the launch traced here: 264 us
  waiting for transfers between devices  165 us (62%)
  matrix products  34.7 us (13%)
  starting transfers between devices  30.9 us (12%)
  between operations  13.2 us (5%)
  local copies, waits for them, and re-layouts  10.8 us (4%)
  blocking collectives  8.61 us (3%)
    all_to_all x1, waiting for transfers between devices, per_device(): lax.all_to_all(packed_rows, 'expert', split_axis=0, concat_axis=0, tiled=...  43.4 us
    reduce_scatter x1, waiting for transfers between devices, per_device(): lax.psum_scatter(partial_sum.reshape(experts, tensor_size * capacity, mod...  29.1 us
    all_gather x1, waiting for transfers between devices, per_device(): lax.all_gather(out_grads, 'tensor', axis=1, tiled=True)  28.9 us
    all_gather x1, waiting for transfers between devices, per_device(): lax.all_gather(tokens, 'tensor', axis=1, tiled=True)  26.7 us
    all_to_all x1, waiting for transfers between devices, per_device(): lax.all_to_all(packed_grads, 'expert', split_axis=0, concat_axis=0, tiled...  17.8 us
    all_to_all x1, waiting for transfers between devices, per_device(): lax.all_to_all(summed, 'expert', split_axis=0, concat_axis=0, tiled=True)  17.7 us
    all_to_all x1, starting transfers between devices, per_device(): lax.all_to_all(packed_grads, 'expert', split_axis=0, concat_axis=0, tiled...  12.7 us
    dot_general x1, matrix products, expert_partial(): lax.dot_general(gate_grad, gate_matrix, contract, preferred_element_type=...  11.5 us
  transfers between devices with their start and end apart: 6, of which 6 were waited for; matrix products, arithmetic and copies ran while one was open for 4% of the time, Pallas kernels for 0%

commit v1 on v0

v1 whole, which is shorter than its diff:
```python
import functools

import jax
import jax.numpy as jnp
from jax import lax
from jax.experimental import pallas as pl
from jax.experimental.pallas import tpu as pltpu
from jax.sharding import PartitionSpec as P

MESH = pl.DeviceIdType.MESH
F32 = jnp.float32
BF16 = jnp.bfloat16
OFFSETS = (0, 1, -1, 2, -2, 3, -3, 4)
PLANES = 8
MEMBERS = 8
NT = (((1,), (1,)), ((), ()))
TN = (((0,), (0,)), ((), ()))


def place_of(species, table_ref, my_plane, experts, capacity, block):
    count = species.shape[1]
    expert_of = jnp.zeros_like(species)
    for kind in range(experts):
        expert_of = jnp.where(species == kind, table_ref[kind], expert_of)
    ids = lax.broadcasted_iota(jnp.int32, (experts, count), 0)
    hits = ids == expert_of
    before = lax.broadcasted_iota(jnp.int32, (count, count), 0)
    after = lax.broadcasted_iota(jnp.int32, (count, count), 1)
    same_block = (before // block) == (after // block)
    earlier_of = jnp.where((before < after) & same_block, 1.0, 0.0).astype(BF16)
    hits_f = jnp.where(hits, 1.0, 0.0)
    earlier = jnp.dot(hits_f.astype(BF16), earlier_of, preferred_element_type=F32)
    slot = jnp.sum(hits_f * earlier, axis=0, keepdims=True).astype(jnp.int32)
    plane = expert_of // MEMBERS
    away = (plane - my_plane + PLANES) % PLANES
    half = PLANES // 2
    chunk = jnp.where(away == 0, 0, jnp.where(away <= half, 2 * away - 1, 2 * (PLANES - away)))
    chunk = jnp.minimum(chunk, PLANES - 1)
    block_id = lax.broadcasted_iota(jnp.int32, (1, count), 1) // block
    blocks = count // block
    return (chunk * MEMBERS + expert_of % MEMBERS) * (blocks * capacity) + block_id * capacity + slot


def kernel(
    capacity,
    tokens_ref, grads_ref, species_ref, table_ref, gate_hbm, up_hbm, down_hbm,
    out_ref,
    pack, xin, rows, rgrads, gate_w, up_w, down_w, gate_g, up_g,
    send_far, send_near, recv_far, recv_near, sums, ret, select,
    w_sem, a_send, a_recv, y_send, y_recv, o_send, o_recv, f_send, f_recv, n_send, n_recv, r_send, r_recv,
):
    experts = lax.axis_size("expert")
    tensor_size = lax.axis_size("tensor")
    me = lax.axis_index("expert")
    mine = lax.axis_index("tensor")
    my_plane = me // MEMBERS
    my_member = me % MEMBERS
    right = (mine + 1) % tensor_size
    left = (mine + tensor_size - 1) % tensor_size
    width = tokens_ref.shape[1]
    half_slots = experts // 2
    half_rows = half_slots * 8

    feature = (mine, left, right, (mine + 2) % tensor_size)
    weight_copies = []
    for j in range(4):
        start = pl.multiple_of(feature[j] * width, width)
        for w, (src, dst) in enumerate((
            (gate_hbm.at[pl.ds(start, width), :], gate_w.at[pl.ds(j * width, width), :]),
            (up_hbm.at[pl.ds(start, width), :], up_w.at[pl.ds(j * width, width), :]),
            (down_hbm.at[:, pl.ds(start, width)], down_w.at[:, pl.ds(j * width, width)]),
        )):
            copy = pltpu.make_async_copy(src, dst, w_sem.at[w, j])
            copy.start()
            weight_copies.append(copy)

    def device(offset, member):
        plane = (my_plane + offset + PLANES) % PLANES
        return (plane * MEMBERS + member, mine)

    barrier = pltpu.get_barrier_semaphore()
    for c in range(PLANES):
        for r in range(MEMBERS):
            if c == 0 and r == 0:
                continue
            pl.semaphore_signal(barrier, inc=1, device_id=device(OFFSETS[c], (my_member + r) % MEMBERS), device_id_type=MESH)
    for side in (left, right):
        pl.semaphore_signal(barrier, inc=1, device_id=(me, side), device_id_type=MESH)

    block = tokens_ref.shape[0] // tensor_size
    place = place_of(species_ref[...], table_ref, my_plane, experts, capacity, block)
    slot_rows = tensor_size * capacity
    slot_ids = lax.broadcasted_iota(jnp.int32, (experts * slot_rows, place.shape[1]), 0)
    chosen = jnp.where(slot_ids == place, 1.0, 0.0).astype(BF16)
    select[...] = chosen

    def pack_chunk(c):
        part = select[pl.ds(c * 64, 64), :]
        own_rows = jnp.dot(part, tokens_ref[...], preferred_element_type=F32)
        own_grads = jnp.dot(part, grads_ref[...], preferred_element_type=F32)
        both = jnp.concatenate(
            [own_rows.reshape(MEMBERS, 8, width), own_grads.reshape(MEMBERS, 8, width)], axis=1
        )
        pack[pl.ds(c * MEMBERS, MEMBERS)] = both.astype(BF16)

    for c in range(PLANES):
        pack_chunk(c)
    pl.semaphore_wait(barrier, experts - 1 + 2)

    def a_copy(c, member, target):
        return pltpu.make_async_remote_copy(
            src_ref=pack.at[c * MEMBERS + member],
            dst_ref=xin.at[0, c * MEMBERS + my_member],
            send_sem=a_send.at[c],
            recv_sem=a_recv.at[c],
            device_id=target,
            device_id_type=MESH,
        )

    pltpu.make_async_copy(pack.at[my_member], xin.at[0, my_member], a_recv.at[0]).start()
    for c in range(PLANES):
        for r in range(MEMBERS):
            if c == 0 and r == 0:
                continue
            member = (my_member + r) % MEMBERS
            a_copy(c, member, device(OFFSETS[c], member)).start()

    def span(c):
        return pl.ds(c * MEMBERS, MEMBERS)

    def y_copy(side, c):
        return pltpu.make_async_remote_copy(
            src_ref=xin.at[0, span(c)],
            dst_ref=xin.at[1 + side, span(c)],
            send_sem=y_send.at[side, c],
            recv_sem=y_recv.at[side, c],
            device_id=(me, (right, left)[side]),
            device_id_type=MESH,
        )

    def o_copy(side, c):
        part = pl.ds(c * MEMBERS + side * (MEMBERS // 2), MEMBERS // 2)
        return pltpu.make_async_remote_copy(
            src_ref=xin.at[1 + side, part],
            dst_ref=xin.at[3, part],
            send_sem=o_send.at[side, c],
            recv_sem=o_recv.at[side, c],
            device_id=(me, (right, left)[side]),
            device_id_type=MESH,
        )

    def gather_first(c):
        pltpu.make_async_copy(pack.at[span(c)], xin.at[0, span(c)], a_recv.at[c]).wait()
        for side in range(2):
            y_copy(side, c).start()

    def gather_relay(c):
        for side in range(2):
            y_copy(side, c).wait_recv()
            o_copy(side, c).start()

    def gather_last(c):
        for side in range(2):
            o_copy(side, c).wait_recv()

    def unpack_chunks(first, count):
        for j in range(4):
            both = xin[j, pl.ds(first * MEMBERS, count * MEMBERS)].astype(F32)
            at = pl.ds(first * 64, count * 64)
            rows[at, pl.ds(j * width, width)] = both[:, 0:8, :].reshape(count * 64, width).astype(BF16)
            rgrads[at, pl.ds(j * width, width)] = both[:, 8:16, :].reshape(count * 64, width).astype(BF16)

    def forward(h):
        at = pl.ds(h * half_rows, half_rows)

        @pl.loop(0, gate_w.shape[1] // 256)
        def _(n):
            cols = pl.ds(pl.multiple_of(n * 256, 256), 256)
            x = rows[at, :]
            gate = jnp.dot(x, gate_w[:, cols], preferred_element_type=F32)
            up = jnp.dot(x, up_w[:, cols], preferred_element_type=F32)
            hidden = lax.dot_general(rgrads[at, :], down_w[cols, :], NT, preferred_element_type=F32)
            s = jax.nn.sigmoid(gate)
            hs = hidden * s
            up_g[h, :, cols] = (hs * gate).astype(BF16)
            gate_g[h, :, cols] = (hs * up * (1.0 + gate * (1.0 - s))).astype(BF16)

    def partial(h, j):
        feats = pl.ds(j * width, width)
        return lax.dot_general(gate_g[h], gate_w[feats, :], NT, preferred_element_type=F32) + lax.dot_general(
            up_g[h], up_w[feats, :], NT, preferred_element_type=F32
        )

    quarter = half_rows // 2

    def far_copy(side, h):
        return pltpu.make_async_remote_copy(
            src_ref=send_far.at[h, side],
            dst_ref=recv_far.at[h, side],
            send_sem=f_send.at[h, side],
            recv_sem=f_recv.at[h, side],
            device_id=(me, (right, left)[side]),
            device_id_type=MESH,
        )

    def near_copy(side, h):
        return pltpu.make_async_remote_copy(
            src_ref=send_near.at[h, side],
            dst_ref=recv_near.at[h, side],
            send_sem=n_send.at[h, side],
            recv_sem=n_recv.at[h, side],
            device_id=(me, (right, left)[side]),
            device_id_type=MESH,
        )

    def scatter_far(h):
        far = partial(h, 3).astype(BF16)
        for side in range(2):
            send_far[h, side] = far[side * quarter:(side + 1) * quarter]
            far_copy(side, h).start()

    def scatter_near(h):
        for side in range(2):
            near = partial(h, 2 - side)
            far_copy(side, h).wait_recv()
            arrived = recv_far[h, side].astype(F32)
            mid = (near[:quarter], near[quarter:])
            parts = [mid[0], mid[1]]
            parts[side] = parts[side] + arrived
            for i in range(2):
                send_near[h, side, pl.ds(i * quarter, quarter)] = parts[i].astype(BF16)
            near_copy(side, h).start()

    def r_copy(c, member, target):
        return pltpu.make_async_remote_copy(
            src_ref=sums.at[c * MEMBERS + member],
            dst_ref=ret.at[c * MEMBERS + my_member],
            send_sem=r_send.at[c // 4],
            recv_sem=r_recv.at[c // 4],
            device_id=target,
            device_id_type=MESH,
        )

    def scatter_own(h):
        own = partial(h, 0)
        for side in range(2):
            near_copy(side, h).wait_recv()
            own = own + recv_near[h, side].astype(F32)
        sums[pl.ds(h * half_slots, half_slots)] = own.reshape(half_slots, 8, width).astype(BF16)
        if h == 0:
            pltpu.make_async_copy(sums.at[my_member], ret.at[my_member], r_recv.at[0]).start()
        for c in range(4 * h, 4 * h + 4):
            for r in range(MEMBERS):
                if c == 0 and r == 0:
                    continue
                member = (my_member + r) % MEMBERS
                r_copy(c, member, device(-OFFSETS[c], member)).start()

    for step in range(PLANES + 2):
        if step < PLANES:
            gather_first(step)
        if 0 <= step - 1 < PLANES:
            gather_relay(step - 1)
        if 0 <= step - 2 < PLANES:
            gather_last(step - 2)
    for copy in weight_copies:
        copy.wait()
    for h in range(2):
        unpack_chunks(4 * h, 4)
        forward(h)
        scatter_far(h)
        scatter_near(h)
        scatter_own(h)

    for h in range(2):
        at = pl.ds(h * half_slots, half_slots)
        pltpu.make_async_copy(sums.at[at], ret.at[at], r_recv.at[h]).wait()
    back = ret[...].astype(F32).reshape(experts * 8, width).astype(BF16)
    out_ref[...] = lax.dot_general(select[...], back, TN, preferred_element_type=F32).astype(BF16)

    for c in range(PLANES):
        count = MEMBERS - 1 if c == 0 else MEMBERS
        at = pl.ds(c * MEMBERS, count)
        pltpu.make_async_copy(pack.at[at], xin.at[0, at], a_send.at[c]).wait()
    for c in range(PLANES):
        for side in range(2):
            y_copy(side, c).wait_send()
            o_copy(side, c).wait_send()
    for h in range(2):
        for side in range(2):
            far_copy(side, h).wait_send()
            near_copy(side, h).wait_send()
        count = half_slots - 1 if h == 0 else half_slots
        at = pl.ds(h * half_slots, count)
        pltpu.make_async_copy(sums.at[at], ret.at[at], r_send.at[h]).wait()


def per_device(tokens, out_grads, species, expert_table, gate_weight, up_weight, down_weight):
    experts = expert_table.shape[0]
    tensor_size = lax.axis_size("tensor")
    count, width = tokens.shape
    capacity = 2 * (count // tensor_size) // experts
    depth, hidden = gate_weight.shape[1:]
    all_rows = experts * tensor_size * capacity
    vmem = pl.BlockSpec(memory_space=pltpu.VMEM)
    hbm = pl.BlockSpec(memory_space=pl.ANY)
    dma = pltpu.SemaphoreType.DMA
    return pl.pallas_call(
        functools.partial(kernel, capacity),
        out_shape=jax.ShapeDtypeStruct((count, width), BF16),
        in_specs=[vmem, vmem, vmem, pl.BlockSpec(memory_space=pltpu.SMEM), hbm, hbm, hbm],
        out_specs=vmem,
        scratch_shapes=[
            pltpu.VMEM((experts, 16, width), BF16),
            pltpu.VMEM((tensor_size, experts, 16, width), BF16),
            pltpu.VMEM((all_rows, depth), BF16),
            pltpu.VMEM((all_rows, depth), BF16),
            pltpu.VMEM((depth, hidden), BF16),
            pltpu.VMEM((depth, hidden), BF16),
            pltpu.VMEM((hidden, depth), BF16),
            pltpu.VMEM((2, all_rows // 2, hidden), BF16),
            pltpu.VMEM((2, all_rows // 2, hidden), BF16),
            pltpu.VMEM((2, 2, all_rows // 4, width), BF16),
            pltpu.VMEM((2, 2, all_rows // 2, width), BF16),
            pltpu.VMEM((2, 2, all_rows // 4, width), BF16),
            pltpu.VMEM((2, 2, all_rows // 2, width), BF16),
            pltpu.VMEM((experts, 8, width), BF16),
            pltpu.VMEM((experts, 8, width), BF16),
            pltpu.VMEM((all_rows, count), BF16),
            dma((3, 4)), dma((8,)), dma((8,)), dma((2, 8)), dma((2, 8)), dma((2, 8)), dma((2, 8)),
            dma((2, 2)), dma((2, 2)), dma((2, 2)), dma((2, 2)), dma((2,)), dma((2,)),
        ],
        compiler_params=pltpu.CompilerParams(
            collective_id=0, has_side_effects=True, vmem_limit_bytes=56 * 1024 * 1024
        ),
    )(tokens, out_grads, species.reshape(1, count), expert_table, gate_weight[0], up_weight[0], down_weight[0])


def solution(mesh):
    placed = (
        P("expert", "tensor"),
        P("expert", "tensor"),
        P("expert", None),
        P(),
        P("expert", None, "tensor"),
        P("expert", None, "tensor"),
        P("expert", "tensor", None),
    )
    return jax.shard_map(
        per_device, mesh=mesh, in_specs=placed, out_specs=P("expert", "tensor"), check_vma=False
    )
```

time: 265 us -> 106 us (0.40)
  waiting for transfers between devices: 165 us -> 0 us
  Pallas kernels: 0 us -> 103 us
  matrix products: 34.7 us -> 0 us
  starting transfers between devices: 30.9 us -> 0 us
  between operations: 13.2 us -> 0.01 us
  local copies, waits for them, and re-layouts: 10.8 us -> 1.67 us
  blocking collectives: 8.61 us -> 0 us
    pallas_call x0 -> x1, Pallas kernels: none -> 103 us  [per_device(): pl.pallas_call(functools.partial(kernel, capacity), out_shape=jax.ShapeDt...]
    all_to_all x3 -> x0, waiting for transfers between devices: 78.9 us -> none  [the longest x1 43.4 us: per_device(): lax.all_to_all(packed_rows, 'expert', split_axis=0, concat_axis=0, tiled=...]
    all_gather x2 -> x0, waiting for transfers between devices: 55.6 us -> none  [the longest x1 28.9 us: per_device(): lax.all_gather(out_grads, 'tensor', axis=1, tiled=True)]
    dot_general x7 -> x0, matrix products: 34.7 us -> none  [the longest x1 11.5 us: expert_partial(): lax.dot_general(gate_grad, gate_matrix, contract, preferred_element_type=...]
    all_to_all x3 -> x0, starting transfers between devices: 30.6 us -> none  [the longest x1 12.7 us: per_device(): lax.all_to_all(packed_grads, 'expert', split_axis=0, concat_axis=0, tiled...]
    reduce_scatter x1 -> x0, waiting for transfers between devices: 29.1 us -> none  [per_device(): lax.psum_scatter(partial_sum.reshape(experts, tensor_size * capacity, mod...]
    all_to_all x1 -> x0, blocking collectives: 8.61 us -> none  [per_device(): lax.all_to_all(own_grads, 'tensor', split_axis=1, concat_axis=0, tiled=True)]
    reshape x4 -> x0, local copies, waits for them, and re-layouts: 5.22 us -> none  [the longest x1 2.48 us: per_device(): packed_rows.reshape(experts, tensor_size * capacity, model_width)]
  transfers between devices with their start and end apart: 6 -> 0, of which waited for: 6 -> 0; matrix products, arithmetic and copies ran while one was open for 4% -> 0% of each run, Pallas kernels for 0% -> 0%
where the time goes in v1:
time: 106 us; the launch traced here: 104 us
  Pallas kernels  103 us (97%)
  local copies, waits for them, and re-layouts  1.67 us (2%)
    pallas_call x1, Pallas kernels, per_device(): pl.pallas_call(functools.partial(kernel, capacity), out_shape=jax.ShapeDt...  103 us

profile of v1, /device:TPU:1, one launch (start us, length us, event | category | flops | bytes accessed | tf_op | source)
XLA Modules:
  0.0 104.3 jit_solution(14090304565219518955)
XLA Ops:
  0.0 102.7 %shard_map.73 = bf16[256,512]{1,0:T(8,128)(2,1)} custom-call(bf16[256,512]{1,0:T(8,128)(2,1)} %tokens_ref.1, bf16[256,512]{1,0:T(8,128)(2,1)} %grads_ref.1, s32[1,256]{1,0:T(1,128)} %bitcast.7, s32[64]{0:T(128)} %table_ref.1, bf16[2048,1024]{1,0:T(8,128)(2,1)} %bitcast.4, bf16[2048,1024]{1,0:T(8,128)(2,1)} %bitcast.5, bf16[1024,2048]{1,0:T(8,128)(2,1)} %bitcast.6), custom_call_target="tpu_custom_call" | custom-call | tf_op jit(solution)/shard_map/pallas_call | solution.py:308
  102.7 1.7 %copy.9 = bf16[256,512]{1,0:T(8,128)(2,1)} copy(bf16[256,512]{1,0:T(8,128)(2,1)} %shard_map.73) | data formatting | bytes 524288

commit v2 on v0

v2 whole, which is shorter than its diff:
```python
import functools

import jax
import jax.numpy as jnp
from jax import lax
from jax.experimental import pallas as pl
from jax.experimental.pallas import tpu as pltpu
from jax.sharding import PartitionSpec as P

MESH = pl.DeviceIdType.MESH
F32 = jnp.float32
BF16 = jnp.bfloat16
NT = (((1,), (1,)), ((), ()))
PLANES, ACROSS, CORES = 8, 4, 2
CHIPS = (
    (0, 0),
    (0, 1), (0, -1), (1, 0),
    (-1, 0), (1, 1), (-1, -1), (1, -1),
    (3, 0), (-3, 0), (4, 0), (-1, 1),
    (3, 1), (-3, -1), (4, 1), (0, 2),
    (3, -1), (-3, 1), (4, -1), (2, 2),
    (3, 2), (-3, 2), (4, 2), (-2, 2),
    (2, 0), (-2, 0), (1, 2), (-1, 2),
    (2, 1), (-2, -1), (2, -1), (-2, 1),
)
UNITS = ((0, 2), (2, 6), (8, 8), (16, 8), (24, 8), (32, 8), (40, 8), (48, 8), (56, 8))
GROUPS = ((0, 32), (32, 16), (48, 16))
ROWS = 8
TILE = 512


def place_of(species, table_ref, my_plane, my_across, experts, capacity, block):
    count = species.shape[1]
    expert_of = jnp.zeros_like(species)
    for kind in range(experts):
        expert_of = jnp.where(species == kind, table_ref[kind], expert_of)
    ids = lax.broadcasted_iota(jnp.int32, (experts, count), 0)
    hits = jnp.where(ids == expert_of, 1.0, 0.0)
    before = lax.broadcasted_iota(jnp.int32, (count, count), 0)
    after = lax.broadcasted_iota(jnp.int32, (count, count), 1)
    same_block = (before // block) == (after // block)
    earlier_of = jnp.where((before < after) & same_block, 1.0, 0.0).astype(BF16)
    earlier = jnp.dot(hits.astype(BF16), earlier_of, preferred_element_type=F32)
    slot = jnp.sum(hits * earlier, axis=0, keepdims=True).astype(jnp.int32)
    away = (expert_of // (ACROSS * CORES) - my_plane + PLANES) % PLANES
    aside = ((expert_of // CORES) % ACROSS - my_across + ACROSS) % ACROSS
    step = away * ACROSS + aside
    chip = jnp.zeros_like(step)
    for k in range(1, len(CHIPS)):
        chip = jnp.where(step == (CHIPS[k][0] % PLANES) * ACROSS + CHIPS[k][1] % ACROSS, k, chip)
    block_id = lax.broadcasted_iota(jnp.int32, (1, count), 1) // block
    return (chip * CORES + expert_of % CORES) * ROWS + block_id * capacity + slot


def kernel(
    capacity,
    tokens_hbm, grads_hbm, species_hbm, table_ref, gate_hbm, up_hbm, down_hbm,
    ret, place_hbm,
    tokens_ref, grads_ref, species_ref, place_ref,
    pack, xin, rows, rgrads, early, gate_w, up_w, down_w, gate_g, up_g,
    send_far, send_near, recv_far, recv_near, sums,
    i_sem, p_sem, w_sem, a_send, a_recv, y_send, y_recv, o_send, o_recv, f_send, f_recv, n_send, n_recv, r_send, r_recv,
):
    experts = lax.axis_size("expert")
    tensor_size = lax.axis_size("tensor")
    me = lax.axis_index("expert")
    mine = lax.axis_index("tensor")
    my_plane = me // (ACROSS * CORES)
    my_across = (me // CORES) % ACROSS
    my_core = me % CORES
    right = (mine + 1) % tensor_size
    left = (mine + tensor_size - 1) % tensor_size
    width = tokens_ref.shape[1]

    def device(k, core, way=1):
        plane = (my_plane + way * CHIPS[k][0] + PLANES) % PLANES
        across = (my_across + way * CHIPS[k][1] + ACROSS) % ACROSS
        return ((plane * ACROSS + across) * CORES + core, mine)

    def cores(k):
        return (1 - my_core,) if k == 0 else (my_core, 1 - my_core)

    barrier = pltpu.get_barrier_semaphore()
    for k in reversed(range(len(CHIPS))):
        for core in cores(k):
            pl.semaphore_signal(barrier, inc=1, device_id=device(k, core), device_id_type=MESH)
    for side in (left, right):
        pl.semaphore_signal(barrier, inc=1, device_id=(me, side), device_id_type=MESH)

    inputs = [
        pltpu.make_async_copy(src, dst, i_sem.at[i])
        for i, (src, dst) in enumerate(((species_hbm, species_ref), (tokens_hbm, tokens_ref), (grads_hbm, grads_ref)))
    ]
    for copy in inputs:
        copy.start()
    inputs[0].wait()
    block = tokens_ref.shape[0] // tensor_size
    place = place_of(species_ref[...], table_ref, my_plane, my_across, experts, capacity, block)
    place_ref[...] = place
    place_out = pltpu.make_async_copy(place_ref, place_hbm, p_sem)
    place_out.start()
    inputs[1].wait()
    inputs[2].wait()

    for c in range(experts // 8):
        ids = lax.broadcasted_iota(jnp.int32, (8 * ROWS, place.shape[1]), 0) + c * 8 * ROWS
        part = jnp.where(ids == place, 1.0, 0.0).astype(BF16)
        own_rows = jnp.dot(part, tokens_ref[...], preferred_element_type=F32)
        own_grads = jnp.dot(part, grads_ref[...], preferred_element_type=F32)
        both = jnp.concatenate(
            [own_rows.reshape(8, ROWS, width), own_grads.reshape(8, ROWS, width)], axis=1
        )
        pack[pl.ds(c * 8, 8)] = both.astype(BF16)
    pl.semaphore_wait(barrier, experts - 1 + 2)

    def a_start(u):
        first, count = UNITS[u]
        for k in range(first // CORES, (first + count) // CORES):
            for core in cores(k):
                pltpu.make_async_remote_copy(
                    src_ref=pack.at[k * CORES + core],
                    dst_ref=xin.at[0, k * CORES + my_core],
                    send_sem=a_send.at[u],
                    recv_sem=a_recv.at[u],
                    device_id=device(k, core),
                    device_id_type=MESH,
                ).start()

    def span(u):
        return pl.ds(*UNITS[u])

    def y_copy(side, u):
        return pltpu.make_async_remote_copy(
            src_ref=xin.at[0, span(u)],
            dst_ref=xin.at[1 + side, span(u)],
            send_sem=y_send.at[side, u],
            recv_sem=y_recv.at[side, u],
            device_id=(me, (right, left)[side]),
            device_id_type=MESH,
        )

    def o_copy(side, u):
        first, count = UNITS[u]
        part = pl.ds(first + side * (count // 2), count // 2)
        return pltpu.make_async_remote_copy(
            src_ref=xin.at[1 + side, part],
            dst_ref=xin.at[3, part],
            send_sem=o_send.at[side, u],
            recv_sem=o_recv.at[side, u],
            device_id=(me, (right, left)[side]),
            device_id_type=MESH,
        )

    def gather_first(u):
        pltpu.make_async_copy(pack.at[span(u)], xin.at[0, span(u)], a_recv.at[u]).wait()
        for side in range(2):
            y_copy(side, u).start()

    def gather_relay(u):
        for side in range(2):
            y_copy(side, u).wait_recv()
            o_copy(side, u).start()

    def gather_last(u):
        for side in range(2):
            o_copy(side, u).wait_recv()

    def rows_of(g):
        first, count = GROUPS[g]
        return pl.ds(first * ROWS, count * ROWS)

    def split_rows(g, features):
        first, count = GROUPS[g]
        for j in features:
            both = xin[j, pl.ds(first, count)].astype(F32)
            cols = pl.ds(j * width, width)
            rows[rows_of(g), cols] = both[:, 0:ROWS, :].reshape(count * ROWS, width).astype(BF16)
            rgrads[rows_of(g), cols] = both[:, ROWS:2 * ROWS, :].reshape(count * ROWS, width).astype(BF16)

    def products(g, n, first, count):
        at = rows_of(g)
        cols = pl.ds(n * TILE, TILE)
        depth = pl.ds(first * width, count * width)
        x = rows[at, depth]
        gate = jnp.dot(x, gate_w[depth, cols], preferred_element_type=F32)
        up = jnp.dot(x, up_w[depth, cols], preferred_element_type=F32)
        hidden = lax.dot_general(rgrads[at, depth], down_w[cols, depth], NT, preferred_element_type=F32)
        return gate, up, hidden

    def finish(g, n, gate, up, hidden):
        at = rows_of(g)
        cols = pl.ds(n * TILE, TILE)
        s = jax.nn.sigmoid(gate)
        hs = hidden * s
        up_g[at, cols] = (hs * gate).astype(BF16)
        gate_g[at, cols] = (hs * up * (1.0 + gate * (1.0 - s))).astype(BF16)

    def forward(g, n):
        finish(g, n, *products(g, n, 0, 4))

    def forward_part(n):
        for i, value in enumerate(products(len(GROUPS) - 1, n, 0, 3)):
            early[i, :, pl.ds(n * TILE, TILE)] = value

    def forward_end(n):
        g = len(GROUPS) - 1
        late = products(g, n, 3, 1)
        finish(g, n, *(early[i, :, pl.ds(n * TILE, TILE)] + late[i] for i in range(3)))

    def partial(g, j):
        feats = pl.ds(j * width, width)
        at = rows_of(g)
        return lax.dot_general(gate_g[at, :], gate_w[feats, :], NT, preferred_element_type=F32) + lax.dot_general(
            up_g[at, :], up_w[feats, :], NT, preferred_element_type=F32
        )

    def half_of(g):
        first, count = GROUPS[g]
        return pl.ds(first * ROWS // 2, count * ROWS // 2)

    def far_copy(side, g):
        return pltpu.make_async_remote_copy(
            src_ref=send_far.at[side, half_of(g)],
            dst_ref=recv_far.at[side, half_of(g)],
            send_sem=f_send.at[side, g],
            recv_sem=f_recv.at[side, g],
            device_id=(me, (right, left)[side]),
            device_id_type=MESH,
        )

    def near_copy(side, g):
        return pltpu.make_async_remote_copy(
            src_ref=send_near.at[side, rows_of(g)],
            dst_ref=recv_near.at[side, rows_of(g)],
            send_sem=n_send.at[side, g],
            recv_sem=n_recv.at[side, g],
            device_id=(me, (right, left)[side]),
            device_id_type=MESH,
        )

    def scatter_far(g):
        half = GROUPS[g][1] * ROWS // 2
        far = partial(g, 3).astype(BF16)
        for side in range(2):
            send_far[side, half_of(g)] = far[side * half:(side + 1) * half]
            far_copy(side, g).start()

    def scatter_near(g):
        first = GROUPS[g][0] * ROWS
        half = GROUPS[g][1] * ROWS // 2
        for side in range(2):
            near = partial(g, 2 - side)
            far_copy(side, g).wait_recv()
            parts = [near[:half], near[half:]]
            parts[side] = parts[side] + recv_far[side, half_of(g)].astype(F32)
            for i in range(2):
                send_near[side, pl.ds(first + i * half, half)] = parts[i].astype(BF16)
            near_copy(side, g).start()

    def scatter_own(g):
        first, count = GROUPS[g]
        own = partial(g, 0)
        for side in range(2):
            near_copy(side, g).wait_recv()
            own = own + recv_near[side, rows_of(g)].astype(F32)
        sums[pl.ds(first, count)] = own.reshape(count, ROWS, width).astype(BF16)
        if g == 0:
            pltpu.make_async_copy(sums.at[my_core], ret.at[my_core], r_recv.at[0]).start()
        for k in range(first // CORES, (first + count) // CORES):
            for core in cores(k):
                pltpu.make_async_remote_copy(
                    src_ref=sums.at[k * CORES + core],
                    dst_ref=ret.at[k * CORES + my_core],
                    send_sem=r_send.at[g],
                    recv_sem=r_recv.at[g],
                    device_id=device(k, core, -1),
                    device_id_type=MESH,
                ).start()

    pltpu.make_async_copy(pack.at[my_core], xin.at[0, my_core], a_recv.at[0]).start()
    for u in range(3):
        a_start(u)
    gather_first(0)
    a_start(3)
    a_start(4)
    gather_first(1)
    for u in range(5, len(UNITS)):
        a_start(u)

    feature = (mine, left, right, (mine + 2) % tensor_size)
    weight_copies = []
    for j in range(4):
        start = pl.multiple_of(feature[j] * width, width)
        for w, (src, dst) in enumerate((
            (gate_hbm.at[pl.ds(start, width), :], gate_w.at[pl.ds(j * width, width), :]),
            (up_hbm.at[pl.ds(start, width), :], up_w.at[pl.ds(j * width, width), :]),
            (down_hbm.at[:, pl.ds(start, width)], down_w.at[:, pl.ds(j * width, width)]),
        )):
            copy = pltpu.make_async_copy(src, dst, w_sem.at[w, j])
            copy.start()
            weight_copies.append(copy)

    def weights_here():
        for copy in weight_copies:
            copy.wait()

    after = {
        3: (weights_here,),
        5: (lambda: split_rows(0, range(4)), lambda: forward(0, 0)),
        6: (lambda: forward(0, 1), lambda: scatter_far(0)),
        7: (
            lambda: scatter_near(0), lambda: split_rows(1, range(4)), lambda: forward(1, 0), lambda: forward(1, 1),
            lambda: scatter_far(1),
        ),
        8: (
            lambda: split_rows(2, range(3)), lambda: forward_part(0), lambda: forward_part(1),
            lambda: scatter_near(1),
        ),
    }
    for u in range(len(UNITS)):
        if u >= 1 and u + 1 < len(UNITS):
            gather_first(u + 1)
        gather_relay(u)
        if u >= 1:
            gather_last(u - 1)
        for task in after.get(u, ()):
            task()
    gather_last(len(UNITS) - 1)
    split_rows(2, (3,))
    forward_end(0)
    forward_end(1)
    scatter_far(2)
    scatter_own(0)
    scatter_near(2)
    scatter_own(1)
    scatter_own(2)

    place_out.wait()
    for u in range(len(UNITS)):
        first, count = UNITS[u]
        at = pl.ds(first, count - 1 if u == 0 else count)
        pltpu.make_async_copy(pack.at[at], xin.at[0, at], a_send.at[u]).wait()
        for side in range(2):
            y_copy(side, u).wait_send()
            o_copy(side, u).wait_send()
    for g in range(len(GROUPS)):
        for side in range(2):
            far_copy(side, g).wait_send()
            near_copy(side, g).wait_send()
        first, count = GROUPS[g]
        at = pl.ds(first, count - 1 if g == 0 else count)
        pltpu.make_async_copy(sums.at[at], ret.at[at], r_send.at[g]).wait()
    for g in range(len(GROUPS)):
        at = pl.ds(*GROUPS[g])
        pltpu.make_async_copy(sums.at[at], ret.at[at], r_recv.at[g]).wait()


def per_device(tokens, out_grads, species, expert_table, gate_weight, up_weight, down_weight):
    experts = expert_table.shape[0]
    tensor_size = lax.axis_size("tensor")
    count, width = tokens.shape
    capacity = 2 * (count // tensor_size) // experts
    depth, hidden = gate_weight.shape[1:]
    all_rows = experts * ROWS
    hbm = pl.BlockSpec(memory_space=pl.ANY)
    dma = pltpu.SemaphoreType.DMA
    units, groups = len(UNITS), len(GROUPS)
    returned, place = pl.pallas_call(
        functools.partial(kernel, capacity),
        out_shape=(
            pltpu.VMEM((experts, ROWS, width), BF16),
            jax.ShapeDtypeStruct((1, count), jnp.int32),
        ),
        in_specs=[hbm, hbm, hbm, pl.BlockSpec(memory_space=pltpu.SMEM), hbm, hbm, hbm],
        out_specs=(pl.BlockSpec(memory_space=pltpu.VMEM), hbm),
        scratch_shapes=[
            pltpu.VMEM((count, width), BF16),
            pltpu.VMEM((count, width), BF16),
            pltpu.VMEM((1, count), jnp.int32),
            pltpu.VMEM((1, count), jnp.int32),
            pltpu.VMEM((experts, 2 * ROWS, width), BF16),
            pltpu.VMEM((tensor_size, experts, 2 * ROWS, width), BF16),
            pltpu.VMEM((all_rows, depth), BF16),
            pltpu.VMEM((all_rows, depth), BF16),
            pltpu.VMEM((3, GROUPS[-1][1] * ROWS, hidden), F32),
            pltpu.VMEM((depth, hidden), BF16),
            pltpu.VMEM((depth, hidden), BF16),
            pltpu.VMEM((hidden, depth), BF16),
            pltpu.VMEM((all_rows, hidden), BF16),
            pltpu.VMEM((all_rows, hidden), BF16),
            pltpu.VMEM((2, all_rows // 2, width), BF16),
            pltpu.VMEM((2, all_rows, width), BF16),
            pltpu.VMEM((2, all_rows // 2, width), BF16),
            pltpu.VMEM((2, all_rows, width), BF16),
            pltpu.VMEM((experts, ROWS, width), BF16),
            dma((3,)), dma, dma((3, 4)), dma((units,)), dma((units,)),
            dma((2, units)), dma((2, units)), dma((2, units)), dma((2, units)),
            dma((2, groups)), dma((2, groups)), dma((2, groups)), dma((2, groups)), dma((groups,)), dma((groups,)),
        ],
        compiler_params=pltpu.CompilerParams(
            collective_id=0, has_side_effects=True, vmem_limit_bytes=56 * 1024 * 1024
        ),
    )(tokens, out_grads, species.reshape(1, count), expert_table, gate_weight[0], up_weight[0], down_weight[0])
    ids = lax.broadcasted_iota(jnp.int32, (count, all_rows), 1)
    chosen = (ids == place.reshape(count, 1)).astype(BF16)
    return jnp.dot(chosen, returned.reshape(all_rows, width), preferred_element_type=F32).astype(BF16)


def solution(mesh):
    placed = (
        P("expert", "tensor"),
        P("expert", "tensor"),
        P("expert", None),
        P(),
        P("expert", None, "tensor"),
        P("expert", None, "tensor"),
        P("expert", "tensor", None),
    )
    return jax.shard_map(
        per_device, mesh=mesh, in_specs=placed, out_specs=P("expert", "tensor"), check_vma=False
    )
```

time: 265 us -> 83.6 us (0.32)
  waiting for transfers between devices: 165 us -> 0 us
  Pallas kernels: 0 us -> 81.7 us
  matrix products: 34.7 us -> 1.72 us
  starting transfers between devices: 30.9 us -> 0 us
  between operations: 13.2 us -> 0.01 us
  local copies, waits for them, and re-layouts: 10.8 us -> 0 us
  blocking collectives: 8.61 us -> 0 us
    pallas_call x0 -> x1, Pallas kernels: none -> 81.7 us  [per_device(): pl.pallas_call(functools.partial(kernel, capacity), out_shape=(pltpu.VMEM...]
    all_to_all x3 -> x0, waiting for transfers between devices: 78.9 us -> none  [the longest x1 43.4 us: per_device(): lax.all_to_all(packed_rows, 'expert', split_axis=0, concat_axis=0, tiled=...]
    all_gather x2 -> x0, waiting for transfers between devices: 55.6 us -> none  [the longest x1 28.9 us: per_device(): lax.all_gather(out_grads, 'tensor', axis=1, tiled=True)]
    dot_general x7 -> x1, matrix products: 34.7 us -> 1.72 us  [per_device(): jnp.dot(chosen, returned.reshape(all_rows, width), preferred_element_type...]
    all_to_all x3 -> x0, starting transfers between devices: 30.6 us -> none  [the longest x1 12.7 us: per_device(): lax.all_to_all(packed_grads, 'expert', split_axis=0, concat_axis=0, tiled...]
    reduce_scatter x1 -> x0, waiting for transfers between devices: 29.1 us -> none  [per_device(): lax.psum_scatter(partial_sum.reshape(experts, tensor_size * capacity, mod...]
    all_to_all x1 -> x0, blocking collectives: 8.61 us -> none  [per_device(): lax.all_to_all(own_grads, 'tensor', split_axis=1, concat_axis=0, tiled=True)]
    reshape x4 -> x0, local copies, waits for them, and re-layouts: 5.22 us -> none  [the longest x1 2.48 us: per_device(): packed_rows.reshape(experts, tensor_size * capacity, model_width)]
  transfers between devices with their start and end apart: 6 -> 0, of which waited for: 6 -> 0; matrix products, arithmetic and copies ran while one was open for 4% -> 0% of each run, Pallas kernels for 0% -> 0%
where the time goes in v2:
time: 83.6 us; the launch traced here: 83.4 us
  Pallas kernels  81.7 us (98%)
  matrix products  1.72 us (2%)
    pallas_call x1, Pallas kernels, per_device(): pl.pallas_call(functools.partial(kernel, capacity), out_shape=(pltpu.VMEM...  81.7 us
    dot_general x1, matrix products, per_device(): jnp.dot(chosen, returned.reshape(all_rows, width), preferred_element_type...  1.72 us

profile of v2, /device:TPU:1, one launch (start us, length us, event | category | flops | bytes accessed | tf_op | source)
XLA Modules:
  0.0 83.4 jit_solution(2368699388348352985)
XLA Ops:
  0.0 81.7 %shard_map.73 = (bf16[64,8,512]{2,1,0:T(8,128)(2,1)S(1)}, s32[1,256]{1,0:T(1,128)}) custom-call(bf16[256,512]{1,0:T(8,128)(2,1)} %tokens_hbm.1, bf16[256,512]{1,0:T(8,128)(2,1)} %grads_hbm.1, s32[1,256]{1,0:T(1,128)} %bitcast.11, s32[64]{0:T(128)} %table_ref.1, bf16[2048,1024]{1,0:T(8,128)(2,1)} %bitcast.8, bf16[2048,1024]{1,0:T(8,128)(2,1)} %bitcast.9, ...), custom_call_target="tpu_custom_call" | custom-call | tf_op jit(solution)/shard_map/pallas_call | solution.py:368
  81.7 1.7 %convolution_convert_fusion = bf16[256,512]{1,0:T(8,128)(2,1)} fusion(bf16[64,8,512]{2,1,0:T(8,128)(2,1)S(1)} %get-tuple-element.8, s32[256]{0:T(256)} %bitcast.12), kind=kOutput, calls=%fused_computation | convolution fusion | flops 134479872 | bytes 787456 | tf_op jit(solution)/shard_map/dot_general | solution.py:406

commit v3 on v2

--- a/solution.py
+++ b/solution.py
@@ -54,9 +54,9 @@
 
 def kernel(
     capacity,
-    tokens_hbm, grads_hbm, species_hbm, table_ref, gate_hbm, up_hbm, down_hbm,
+    tokens_hbm, grads_hbm, species_hbm, table_hbm, gate_hbm, up_hbm, down_hbm,
     ret, place_hbm,
-    tokens_ref, grads_ref, species_ref, place_ref,
+    tokens_ref, grads_ref, species_ref, table_ref, place_ref,
     pack, xin, rows, rgrads, early, gate_w, up_w, down_w, gate_g, up_g,
     send_far, send_near, recv_far, recv_near, sums,
     i_sem, p_sem, w_sem, a_send, a_recv, y_send, y_recv, o_send, o_recv, f_send, f_recv, n_send, n_recv, r_send, r_recv,
@@ -89,18 +89,19 @@
 
     inputs = [
         pltpu.make_async_copy(src, dst, i_sem.at[i])
-        for i, (src, dst) in enumerate(((species_hbm, species_ref), (tokens_hbm, tokens_ref), (grads_hbm, grads_ref)))
+        for i, (src, dst) in enumerate(((species_hbm, species_ref), (table_hbm, table_ref), (tokens_hbm, tokens_ref), (grads_hbm, grads_ref)))
     ]
     for copy in inputs:
         copy.start()
     inputs[0].wait()
+    inputs[1].wait()
     block = tokens_ref.shape[0] // tensor_size
     place = place_of(species_ref[...], table_ref, my_plane, my_across, experts, capacity, block)
     place_ref[...] = place
     place_out = pltpu.make_async_copy(place_ref, place_hbm, p_sem)
     place_out.start()
-    inputs[1].wait()
     inputs[2].wait()
+    inputs[3].wait()
 
     for c in range(experts // 8):
         ids = lax.broadcasted_iota(jnp.int32, (8 * ROWS, place.shape[1]), 0) + c * 8 * ROWS
@@ -120,7 +121,7 @@
                 pltpu.make_async_remote_copy(
                     src_ref=pack.at[k * CORES + core],
                     dst_ref=xin.at[0, k * CORES + my_core],
-                    send_sem=a_send.at[u],
+                    send_sem=a_send,
                     recv_sem=a_recv.at[u],
                     device_id=device(k, core),
                     device_id_type=MESH,
@@ -133,7 +134,7 @@
         return pltpu.make_async_remote_copy(
             src_ref=xin.at[0, span(u)],
             dst_ref=xin.at[1 + side, span(u)],
-            send_sem=y_send.at[side, u],
+            send_sem=y_send.at[side],
             recv_sem=y_recv.at[side, u],
             device_id=(me, (right, left)[side]),
             device_id_type=MESH,
@@ -145,7 +146,7 @@
         return pltpu.make_async_remote_copy(
             src_ref=xin.at[1 + side, part],
             dst_ref=xin.at[3, part],
-            send_sem=o_send.at[side, u],
+            send_sem=o_send.at[side],
             recv_sem=o_recv.at[side, u],
             device_id=(me, (right, left)[side]),
             device_id_type=MESH,
@@ -164,6 +165,10 @@
     def gather_last(u):
         for side in range(2):
             o_copy(side, u).wait_recv()
+
+    def arrived(first, end):
+        for u in range(first, end):
+            gather_last(u)
 
     def rows_of(g):
         first, count = GROUPS[g]
@@ -222,7 +227,7 @@
         return pltpu.make_async_remote_copy(
             src_ref=send_far.at[side, half_of(g)],
             dst_ref=recv_far.at[side, half_of(g)],
-            send_sem=f_send.at[side, g],
+            send_sem=f_send.at[side],
             recv_sem=f_recv.at[side, g],
             device_id=(me, (right, left)[side]),
             device_id_type=MESH,
@@ -232,7 +237,7 @@
         return pltpu.make_async_remote_copy(
             src_ref=send_near.at[side, rows_of(g)],
             dst_ref=recv_near.at[side, rows_of(g)],
-            send_sem=n_send.at[side, g],
+            send_sem=n_send.at[side],
             recv_sem=n_recv.at[side, g],
             device_id=(me, (right, left)[side]),
             device_id_type=MESH,
@@ -271,7 +276,7 @@
                 pltpu.make_async_remote_copy(
                     src_ref=sums.at[k * CORES + core],
                     dst_ref=ret.at[k * CORES + my_core],
-                    send_sem=r_send.at[g],
+                    send_sem=r_send,
                     recv_sem=r_recv.at[g],
                     device_id=device(k, core, -1),
                     device_id_type=MESH,
@@ -286,70 +291,59 @@
     gather_first(1)
     for u in range(5, len(UNITS)):
         a_start(u)
+    gather_first(2)
 
     feature = (mine, left, right, (mine + 2) % tensor_size)
-    weight_copies = []
     for j in range(4):
         start = pl.multiple_of(feature[j] * width, width)
-        for w, (src, dst) in enumerate((
-            (gate_hbm.at[pl.ds(start, width), :], gate_w.at[pl.ds(j * width, width), :]),
-            (up_hbm.at[pl.ds(start, width), :], up_w.at[pl.ds(j * width, width), :]),
-            (down_hbm.at[:, pl.ds(start, width)], down_w.at[:, pl.ds(j * width, width)]),
-        )):
-            copy = pltpu.make_async_copy(src, dst, w_sem.at[w, j])
-            copy.start()
-            weight_copies.append(copy)
+        own = pl.ds(j * width, width)
+        pltpu.make_async_copy(gate_hbm.at[pl.ds(start, width), :], gate_w.at[own, :], w_sem.at[0]).start()
+        pltpu.make_async_copy(up_hbm.at[pl.ds(start, width), :], up_w.at[own, :], w_sem.at[1]).start()
+        pltpu.make_async_copy(down_hbm.at[:, pl.ds(start, width)], down_w.at[:, own], w_sem.at[2]).start()
 
     def weights_here():
-        for copy in weight_copies:
-            copy.wait()
+        for i, (src, dst) in enumerate(((gate_hbm, gate_w), (up_hbm, up_w), (down_hbm, down_w))):
+            pltpu.make_async_copy(src, dst, w_sem.at[i]).wait()
 
     after = {
         3: (weights_here,),
-        5: (lambda: split_rows(0, range(4)), lambda: forward(0, 0)),
+        5: (lambda: arrived(0, 5), lambda: split_rows(0, range(4)), lambda: forward(0, 0)),
         6: (lambda: forward(0, 1), lambda: scatter_far(0)),
         7: (
-            lambda: scatter_near(0), lambda: split_rows(1, range(4)), lambda: forward(1, 0), lambda: forward(1, 1),
-            lambda: scatter_far(1),
+            lambda: arrived(5, 7), lambda: split_rows(1, range(4)), lambda: forward(1, 0), lambda: scatter_near(0),
         ),
         8: (
+            lambda: forward(1, 1), lambda: scatter_far(1),
             lambda: split_rows(2, range(3)), lambda: forward_part(0), lambda: forward_part(1),
-            lambda: scatter_near(1),
+            lambda: scatter_own(0),
         ),
     }
     for u in range(len(UNITS)):
-        if u >= 1 and u + 1 < len(UNITS):
+        if u >= 2 and u + 1 < len(UNITS):
             gather_first(u + 1)
         gather_relay(u)
-        if u >= 1:
-            gather_last(u - 1)
         for task in after.get(u, ()):
             task()
-    gather_last(len(UNITS) - 1)
+    arrived(7, 9)
     split_rows(2, (3,))
     forward_end(0)
     forward_end(1)
+    scatter_near(1)
     scatter_far(2)
-    scatter_own(0)
+    scatter_own(1)
     scatter_near(2)
-    scatter_own(1)
     scatter_own(2)
 
     place_out.wait()
-    for u in range(len(UNITS)):
-        first, count = UNITS[u]
-        at = pl.ds(first, count - 1 if u == 0 else count)
-        pltpu.make_async_copy(pack.at[at], xin.at[0, at], a_send.at[u]).wait()
-        for side in range(2):
-            y_copy(side, u).wait_send()
-            o_copy(side, u).wait_send()
-    for g in range(len(GROUPS)):
-        for side in range(2):
-            far_copy(side, g).wait_send()
-            near_copy(side, g).wait_send()
-        first, count = GROUPS[g]
-        at = pl.ds(first, count - 1 if g == 0 else count)
-        pltpu.make_async_copy(sums.at[at], ret.at[at], r_send.at[g]).wait()
+    others = pl.ds(0, experts - 1)
+    pltpu.make_async_copy(pack.at[others], xin.at[0, others], a_send).wait()
+    pltpu.make_async_copy(sums.at[others], ret.at[others], r_send).wait()
+    for side in range(2):
+        relayed = pl.ds(0, experts // 2)
+        pltpu.make_async_copy(xin.at[0], xin.at[1 + side], y_send.at[side]).wait()
+        pltpu.make_async_copy(xin.at[1 + side, relayed], xin.at[3, relayed], o_send.at[side]).wait()
+        pltpu.make_async_copy(send_far.at[side], recv_far.at[side], f_send.at[side]).wait()
+        pltpu.make_async_copy(send_near.at[side], recv_near.at[side], n_send.at[side]).wait()
     for g in range(len(GROUPS)):
         at = pl.ds(*GROUPS[g])
         pltpu.make_async_copy(sums.at[at], ret.at[at], r_recv.at[g]).wait()
@@ -371,12 +365,13 @@
             pltpu.VMEM((experts, ROWS, width), BF16),
             jax.ShapeDtypeStruct((1, count), jnp.int32),
         ),
-        in_specs=[hbm, hbm, hbm, pl.BlockSpec(memory_space=pltpu.SMEM), hbm, hbm, hbm],
+        in_specs=[hbm] * 7,
         out_specs=(pl.BlockSpec(memory_space=pltpu.VMEM), hbm),
         scratch_shapes=[
             pltpu.VMEM((count, width), BF16),
             pltpu.VMEM((count, width), BF16),
             pltpu.VMEM((1, count), jnp.int32),
+            pltpu.SMEM((experts,), jnp.int32),
             pltpu.VMEM((1, count), jnp.int32),
             pltpu.VMEM((experts, 2 * ROWS, width), BF16),
             pltpu.VMEM((tensor_size, experts, 2 * ROWS, width), BF16),
@@ -393,9 +388,9 @@
             pltpu.VMEM((2, all_rows // 2, width), BF16),
             pltpu.VMEM((2, all_rows, width), BF16),
             pltpu.VMEM((experts, ROWS, width), BF16),
-            dma((3,)), dma, dma((3, 4)), dma((units,)), dma((units,)),
-            dma((2, units)), dma((2, units)), dma((2, units)), dma((2, units)),
-            dma((2, groups)), dma((2, groups)), dma((2, groups)), dma((2, groups)), dma((groups,)), dma((groups,)),
+            dma((4,)), dma, dma((3,)), dma, dma((units,)),
+            dma((2,)), dma((2, units)), dma((2,)), dma((2, units)),
+            dma((2,)), dma((2, groups)), dma((2,)), dma((2, groups)), dma, dma((groups,)),
         ],
         compiler_params=pltpu.CompilerParams(
             collective_id=0, has_side_effects=True, vmem_limit_bytes=56 * 1024 * 1024

time: 83.6 us -> 82.2 us (0.983)
  Pallas kernels: 81.7 us -> 80.4 us
    pallas_call x1, Pallas kernels: 81.7 us -> 80.4 us  [per_device(): pl.pallas_call(functools.partial(kernel, capacity), out_shape=(pltpu.VMEM...]
where the time goes in v3:
time: 82.2 us; the launch traced here: 82.1 us
  Pallas kernels  80.4 us (98%)
  matrix products  1.72 us (2%)
    pallas_call x1, Pallas kernels, per_device(): pl.pallas_call(functools.partial(kernel, capacity), out_shape=(pltpu.VMEM...  80.4 us
    dot_general x1, matrix products, per_device(): jnp.dot(chosen, returned.reshape(all_rows, width), preferred_element_type...  1.72 us

profile of v3, /device:TPU:1, one launch (start us, length us, event | category | flops | bytes accessed | tf_op | source)
XLA Modules:
  0.0 82.1 jit_solution(11240234377939318335)
XLA Ops:
  0.0 80.4 %shard_map.73 = (bf16[64,8,512]{2,1,0:T(8,128)(2,1)S(1)}, s32[1,256]{1,0:T(1,128)}) custom-call(bf16[256,512]{1,0:T(8,128)(2,1)} %tokens_hbm.1, bf16[256,512]{1,0:T(8,128)(2,1)} %grads_hbm.1, s32[1,256]{1,0:T(1,128)} %bitcast.11, s32[64]{0:T(128)} %table_hbm.1, bf16[2048,1024]{1,0:T(8,128)(2,1)} %bitcast.8, bf16[2048,1024]{1,0:T(8,128)(2,1)} %bitcast.9, ...), custom_call_target="tpu_custom_call" | custom-call | tf_op jit(solution)/shard_map/pallas_call | solution.py:362
  80.4 1.7 %convolution_convert_fusion = bf16[256,512]{1,0:T(8,128)(2,1)} fusion(bf16[64,8,512]{2,1,0:T(8,128)(2,1)S(1)} %get-tuple-element.8, s32[256]{0:T(256)} %bitcast.12), kind=kOutput, calls=%fused_computation | convolution fusion | flops 134479872 | bytes 787456 | tf_op jit(solution)/shard_map/dot_general | solution.py:401

commit v4 on v3

--- a/solution.py
+++ b/solution.py
@@ -310,12 +310,12 @@
         5: (lambda: arrived(0, 5), lambda: split_rows(0, range(4)), lambda: forward(0, 0)),
         6: (lambda: forward(0, 1), lambda: scatter_far(0)),
         7: (
-            lambda: arrived(5, 7), lambda: split_rows(1, range(4)), lambda: forward(1, 0), lambda: scatter_near(0),
+            lambda: scatter_near(0), lambda: arrived(5, 7), lambda: split_rows(1, range(4)), lambda: forward(1, 0), lambda: forward(1, 1),
+            lambda: scatter_far(1),
         ),
         8: (
-            lambda: forward(1, 1), lambda: scatter_far(1),
             lambda: split_rows(2, range(3)), lambda: forward_part(0), lambda: forward_part(1),
-            lambda: scatter_own(0),
+            lambda: scatter_own(0), lambda: scatter_near(1),
         ),
     }
     for u in range(len(UNITS)):
@@ -328,7 +328,6 @@
     split_rows(2, (3,))
     forward_end(0)
     forward_end(1)
-    scatter_near(1)
     scatter_far(2)
     scatter_own(1)
     scatter_near(2)

time: 82.2 us -> 80.9 us (0.984)
  Pallas kernels: 80.4 us -> 79 us
    pallas_call x1, Pallas kernels: 80.4 us -> 79 us  [per_device(): pl.pallas_call(functools.partial(kernel, capacity), out_shape=(pltpu.VMEM...]
where the time goes in v4:
time: 80.9 us; the launch traced here: 80.8 us
  Pallas kernels  79 us (98%)
  matrix products  1.72 us (2%)
    pallas_call x1, Pallas kernels, per_device(): pl.pallas_call(functools.partial(kernel, capacity), out_shape=(pltpu.VMEM...  79 us
    dot_general x1, matrix products, per_device(): jnp.dot(chosen, returned.reshape(all_rows, width), preferred_element_type...  1.72 us

profile of v4, /device:TPU:1, one launch (start us, length us, event | category | flops | bytes accessed | tf_op | source)
XLA Modules:
  0.0 80.8 jit_solution(3618789617806957224)
XLA Ops:
  0.0 79.0 %shard_map.73 = (bf16[64,8,512]{2,1,0:T(8,128)(2,1)S(1)}, s32[1,256]{1,0:T(1,128)}) custom-call(bf16[256,512]{1,0:T(8,128)(2,1)} %tokens_hbm.1, bf16[256,512]{1,0:T(8,128)(2,1)} %grads_hbm.1, s32[1,256]{1,0:T(1,128)} %bitcast.11, s32[64]{0:T(128)} %table_hbm.1, bf16[2048,1024]{1,0:T(8,128)(2,1)} %bitcast.8, bf16[2048,1024]{1,0:T(8,128)(2,1)} %bitcast.9, ...), custom_call_target="tpu_custom_call" | custom-call | tf_op jit(solution)/shard_map/pallas_call | solution.py:361
  79.0 1.7 %convolution_convert_fusion = bf16[256,512]{1,0:T(8,128)(2,1)} fusion(bf16[64,8,512]{2,1,0:T(8,128)(2,1)S(1)} %get-tuple-element.8, s32[256]{0:T(256)} %bitcast.12), kind=kOutput, calls=%fused_computation | convolution fusion | flops 134479872 | bytes 787456 | tf_op jit(solution)/shard_map/dot_general | solution.py:400

commit v5 on v4

--- a/solution.py
+++ b/solution.py
@@ -271,7 +271,8 @@
         sums[pl.ds(first, count)] = own.reshape(count, ROWS, width).astype(BF16)
         if g == 0:
             pltpu.make_async_copy(sums.at[my_core], ret.at[my_core], r_recv.at[0]).start()
-        for k in range(first // CORES, (first + count) // CORES):
+        chips = sorted(range(first // CORES, (first + count) // CORES), key=lambda k: -sum(map(abs, CHIPS[k])))
+        for k in chips:
             for core in cores(k):
                 pltpu.make_async_remote_copy(
                     src_ref=sums.at[k * CORES + core],

time: 80.9 us -> 81.2 us (level)
  no operation moved by 1% of the time
where the time goes in v5:
time: 81.2 us; the launch traced here: 81 us
  Pallas kernels  79.3 us (98%)
  matrix products  1.72 us (2%)
    pallas_call x1, Pallas kernels, per_device(): pl.pallas_call(functools.partial(kernel, capacity), out_shape=(pltpu.VMEM...  79.3 us
    dot_general x1, matrix products, per_device(): jnp.dot(chosen, returned.reshape(all_rows, width), preferred_element_type...  1.72 us

profile of v5, /device:TPU:1, one launch (start us, length us, event | category | flops | bytes accessed | tf_op | source)
XLA Modules:
  0.0 81.0 jit_solution(14442604452383432335)
XLA Ops:
  0.0 79.3 %shard_map.73 = (bf16[64,8,512]{2,1,0:T(8,128)(2,1)S(1)}, s32[1,256]{1,0:T(1,128)}) custom-call(bf16[256,512]{1,0:T(8,128)(2,1)} %tokens_hbm.1, bf16[256,512]{1,0:T(8,128)(2,1)} %grads_hbm.1, s32[1,256]{1,0:T(1,128)} %bitcast.11, s32[64]{0:T(128)} %table_hbm.1, bf16[2048,1024]{1,0:T(8,128)(2,1)} %bitcast.8, bf16[2048,1024]{1,0:T(8,128)(2,1)} %bitcast.9, ...), custom_call_target="tpu_custom_call" | custom-call | tf_op jit(solution)/shard_map/pallas_call | solution.py:362
  79.3 1.7 %convolution_convert_fusion = bf16[256,512]{1,0:T(8,128)(2,1)} fusion(bf16[64,8,512]{2,1,0:T(8,128)(2,1)S(1)} %get-tuple-element.8, s32[256]{0:T(256)} %bitcast.12), kind=kOutput, calls=%fused_computation | convolution fusion | flops 134479872 | bytes 787456 | tf_op jit(solution)/shard_map/dot_general | solution.py:401
